TPU v7x, 256 devices: a whole 4x4x8 slice. The times are simulated.
256 devices in a mesh: px: 4 (over z_lo), py: 8 (over y, core), ch: 8 (over z_hi, x).
Axes of the slice: x: 4, y: 4, z: 8 (z_hi: 2, z_lo: 4; z = z_hi * 4 + z_lo), core: 2. Of those that a mesh axis runs over, the one named last changes fastest.
Arguments:
- features: bfloat16 [128, 12, 8, 4, 512], P('ch', None, 'py', 'px'), may hold values from -6 to 6
- cotangent: bfloat16 [128, 12, 8, 4, 512], P('ch', None, 'py', 'px'), may hold values from -6 to 6
- weight: bfloat16 [3, 3, 128, 128], replicated, may hold values from -0.1875 to 0.1875
- edge_table: int32 [12, 4, 3], replicated, may hold values from 0 to 11, as said below
- corner_table: int32 [12, 4, 2], replicated, may hold values from 0 to 11, as said below
Outputs:
- activation: bfloat16 [128, 12, 8, 4, 512], P('ch', None, 'py', 'px')
- input_grad: bfloat16 [128, 12, 8, 4, 512], P('ch', None, 'py', 'px')
Inputs may be any that keep to these rules, and one draw needn't show every extreme that they name: edge_table[f, e] = (g, s, r): beyond edge e of face f lie the pixels of side s of face g, in reverse order if r = 1; every side of every face is named exactly once, and if (f, e) names (g, s) then (g, s) names (f, e) with the same r. corner_table[f, c] = (h, q): corner c of face f takes corner pixel q of face h; in each corner column every face appears once, and each q appears 12 times.
All inputs are finite; a program needn't handle non-finite values.
Results may differ from a plain program's by a relative error of at most 0.0049.
Values may be sent and summed in bfloat16 or wider, within the bound.
A program may use at most 192 MiB of HBM per device.

v0:
```python
import jax
import jax.numpy as jnp
from jax import lax
from jax.sharding import PartitionSpec as P

RB = 32


def with_halo(array, sides, width):
    for axis, dim in sides:
        size, length = (lax.axis_size(axis), array.shape[dim])
        up = [(i, (i + 1) % size) for i in range(size - 1)]
        down = [(j, i) for i, j in up]
        last = lax.slice_in_dim(array, length - width, length, axis=dim)
        leading = lax.slice_in_dim(array, 0, width, axis=dim)
        before = lax.ppermute(last, axis, up)
        after = lax.ppermute(leading, axis, down)
        array = jnp.concatenate([before, array, after], axis=dim)
    return array


def edge_strips(lines, edge_table, corner_table):
    chan_count = lines.shape[0]
    face_count = lines.shape[1]
    side_len = lines.shape[3]
    flat_lines = lines.reshape(chan_count, face_count * 4, side_len)
    pixels = jnp.stack(
        [lines[:, :, 0, 0], lines[:, :, 0, -1], lines[:, :, 1, 0], lines[:, :, 1, -1]], axis=2
    ).reshape(chan_count, face_count * 4)
    corner_index = corner_table[:, :, 0] * 4 + corner_table[:, :, 1]
    corner_vals = jnp.take(pixels, corner_index, axis=1)
    strips = []
    for edge_num, start_corner, end_corner in ((0, 0, 1), (1, 2, 3), (2, 0, 2), (3, 1, 3)):
        source_row = edge_table[:, edge_num, 0] * 4 + edge_table[:, edge_num, 1]
        strip_line = jnp.take(flat_lines, source_row, axis=1)
        flipped = (edge_table[:, edge_num, 2] == 1)[None, :, None]
        strip_line = jnp.where(flipped, strip_line[:, :, ::-1], strip_line)
        strips.append(
            jnp.concatenate(
                [
                    corner_vals[:, :, start_corner : start_corner + 1],
                    strip_line,
                    corner_vals[:, :, end_corner : end_corner + 1],
                ],
                axis=2,
            )
        )
    return strips


def face_lines_of(field, row_pos, col_pos, px_count, py_count):
    chan_block = field.shape[0]
    face_count = field.shape[1]
    col_len = field.shape[2]
    row_len = field.shape[3]
    side_len = row_len * px_count
    blank = jnp.zeros((chan_block, face_count, side_len), jnp.float32)

    def placed(values, offset, active):
        return jnp.where(
            active,
            lax.dynamic_update_slice_in_dim(blank, values.astype(jnp.float32), offset, 2),
            0.0,
        )

    contrib = jnp.stack(
        [
            placed(field[:, :, 0, :], row_pos * row_len, col_pos == 0),
            placed(field[:, :, -1, :], row_pos * row_len, col_pos == py_count - 1),
            placed(field[:, :, :, 0], col_pos * col_len, row_pos == 0),
            placed(field[:, :, :, -1], col_pos * col_len, row_pos == px_count - 1),
        ],
        axis=2,
    )
    return lax.psum(contrib.astype(jnp.bfloat16), ("px", "py"))


def pad_field(field, edge_table, corner_table):
    col_len = field.shape[2]
    row_len = field.shape[3]
    row_pos = lax.axis_index("px")
    col_pos = lax.axis_index("py")
    px_count = lax.axis_size("px")
    py_count = lax.axis_size("py")
    padded = with_halo(field, (("px", 3), ("py", 2)), 1)
    lines = face_lines_of(field, row_pos, col_pos, px_count, py_count)
    strips = edge_strips(lines, edge_table, corner_table)
    top_row = lax.dynamic_slice_in_dim(strips[0], row_pos * row_len, row_len + 2, 2)
    bottom_row = lax.dynamic_slice_in_dim(strips[1], row_pos * row_len, row_len + 2, 2)
    left_col = lax.dynamic_slice_in_dim(strips[2], col_pos * col_len, col_len + 2, 2)
    right_col = lax.dynamic_slice_in_dim(strips[3], col_pos * col_len, col_len + 2, 2)
    padded = padded.at[:, :, 0, :].set(jnp.where(col_pos == 0, top_row, padded[:, :, 0, :]))
    padded = padded.at[:, :, -1, :].set(
        jnp.where(col_pos == py_count - 1, bottom_row, padded[:, :, -1, :])
    )
    padded = padded.at[:, :, :, 0].set(jnp.where(row_pos == 0, left_col, padded[:, :, :, 0]))
    padded = padded.at[:, :, :, -1].set(
        jnp.where(row_pos == px_count - 1, right_col, padded[:, :, :, -1])
    )
    return padded


def forward_taps(padded, taps, out_cols, out_rows):
    summed = None
    for tap_row in range(3):
        for tap_col in range(3):
            window = padded[:, :, tap_row : tap_row + out_cols, tap_col : tap_col + out_rows]
            term_val = jnp.einsum(
                "oc,cfab->ofab", taps[tap_row, tap_col], window, preferred_element_type=jnp.float32
            )
            summed = term_val if summed is None else summed + term_val
    return summed


def backward_taps(padded, taps, out_cols, out_rows):
    summed = None
    for tap_row in range(3):
        for tap_col in range(3):
            window = padded[
                :, :, 2 - tap_row : 2 - tap_row + out_cols, 2 - tap_col : 2 - tap_col + out_rows
            ]
            term_val = jnp.einsum(
                "oc,ofab->cfab", taps[tap_row, tap_col], window, preferred_element_type=jnp.float32
            )
            summed = term_val if summed is None else summed + term_val
    return summed


def gate_outputs(preact, cotangent):
    sigmoid_val = jax.nn.sigmoid(preact)
    activation = (preact * sigmoid_val).astype(jnp.bfloat16)
    gated = (
        cotangent.astype(jnp.float32) * sigmoid_val * (1.0 + preact * (1.0 - sigmoid_val))
    ).astype(jnp.bfloat16)
    return (activation, gated)


def local(features, cotangent, weight, edge_table, corner_table):
    chan_block = features.shape[0]
    face_count = features.shape[1]
    tile_len = features.shape[4]
    row_len = RB
    col_len = tile_len // row_len
    features = features.reshape(chan_block, face_count, col_len, row_len)
    cotangent = cotangent.reshape(chan_block, face_count, col_len, row_len)
    ch_pos = lax.axis_index("ch")
    feat_pad = pad_field(features, edge_table, corner_table)
    own_taps = lax.dynamic_slice_in_dim(weight, ch_pos * chan_block, chan_block, 2)
    piece_taps = own_taps
    preact = forward_taps(
        lax.all_gather(feat_pad, "ch", axis=0, tiled=True), piece_taps, col_len, row_len
    )
    activation, gated = gate_outputs(preact, cotangent)
    grad_pad = pad_field(gated, edge_table, corner_table)
    input_taps = lax.dynamic_slice_in_dim(weight, ch_pos * chan_block, chan_block, 3)
    piece_taps = input_taps
    input_grad = backward_taps(
        lax.all_gather(grad_pad, "ch", axis=0, tiled=True), piece_taps, col_len, row_len
    ).astype(jnp.bfloat16)
    out_shape = (chan_block, face_count, 1, 1, tile_len)
    return (activation.reshape(out_shape), input_grad.reshape(out_shape))


def solution(mesh):
    return jax.shard_map(
        local,
        mesh=mesh,
        in_specs=(P("ch", None, "py", "px", None), P("ch", None, "py", "px", None), P(), P(), P()),
        out_specs=(P("ch", None, "py", "px", None), P("ch", None, "py", "px", None)),
        check_vma=False,
    )
```

profile of v0, /device:TPU:8, one launch (start us, length us, event | category | flops | bytes accessed | tf_op | source)
XLA Modules:
  0.0 1055.1 jit_solution(10775510683861696942)
XLA Ops:
  7.2 1.4 reshape.426
  9.9 1.4 convert_select_fusion.2
  11.2 3.0 copy.696
  14.2 1.8 copy.697
  16.1 2.7 select_n.196
  18.7 2.7 select_n.200
  23.1 2.6 copy.698
  27.0 7.1 collective-permute-start
  39.3 1.6 copy.687
  41.3 1.6 copy.689
  43.6 1.9 collective-permute-start.2
  45.5 3.9 collective-permute-start.3
  49.5 1.4 collective-permute-done.3
  51.5 1.6 pad_maximum_fusion
  53.1 254.8 %all-reduce.3.cloned.1.call-done = bf16[16,12,4,128]{1,0,3,2:T(8,128)(2,1)} async-done(((bf16[16,12,4,128]{1,0,3,2:T(8,128)(2,1)}), bf16[16,12,4,128]{1,0,3,2:T(8,128)(2,1)}) %all-reduce.3.cloned.1.call-update) | async-done | bytes 196624 | tf_op jit(solution)/shard_map/psum | solution.py:75
  307.9 3.0 copy.702
  318.9 3.8 scatter.30
  326.8 18.3 %scatter.31 = bf16[16,12,18,34]{3,0,2,1:T(8,128)(2,1)S(1)} dynamic-update-slice(bf16[16,12,18,34]{3,0,2,1:T(8,128)(2,1)S(1)} %scatter.30, bf16[16,12,18,1]{3,0,2,1:T(8,128)(2,1)S(1)} %copy.707, s32[]{:T(128)} %constant.235.clone.1, s32[]{:T(128)} %constant.235.clone.1, s32[]{:T(128)} %constant.235.clone.1, s32[]{:T(128)} %constant.249.clone.1) | dynamic-update-slice | bytes 13828 | tf_op jit(solution)/shard_map/scatter | solution.py:97
  347.9 162.8 %all-gather.3.cloned.1.call-done = bf16[128,12,18,34]{3,0,2,1:T(8,128)(2,1)} async-done(((bf16[16,12,18,34]{3,0,2,1:T(8,128)(2,1)}), bf16[128,12,18,34]{3,0,2,1:T(8,128)(2,1)}) %all-gather.3.cloned.1.call-update) | async-done | bytes 1880080 | tf_op jit(solution)/shard_map/all_gather | solution.py:151
  510.7 4.7 fusion.20
  515.5 1.8 fusion.24
  518.3 1.8 fusion.26
  521.0 1.8 fusion.30
  522.8 1.8 fusion.32
  524.6 2.0 fusion.18
  526.6 2.6 fusion.37
  529.2 1.7 convert_select_fusion.1
  531.6 2.3 copy.725
  536.3 2.2 collective-permute-start.4
  541.1 1.9 select_n.220
  543.0 1.9 select_n.223
  545.7 2.6 copy.727
  551.1 1.9 collective-permute-start.6
  553.0 3.9 collective-permute-start.7
  556.9 1.5 collective-permute-done.7
  559.2 266.2 %all-reduce.5.cloned.1.call-done = bf16[16,12,4,128]{1,0,3,2:T(8,128)(2,1)} async-done(((bf16[16,12,4,128]{1,0,3,2:T(8,128)(2,1)}), bf16[16,12,4,128]{1,0,3,2:T(8,128)(2,1)}) %all-reduce.5.cloned.1.call-update) | async-done | bytes 196624 | tf_op jit(solution)/shard_map/psum | solution.py:75
  825.4 3.0 copy.731
  837.1 3.8 scatter.36
  844.2 18.6 %scatter.39 = bf16[16,12,18,34]{3,0,2,1:T(8,128)(2,1)S(1)} dynamic-update-slice(bf16[16,12,18,34]{3,0,2,1:T(8,128)(2,1)S(1)} %scatter.36, bf16[16,12,18,1]{3,0,2,1:T(8,128)(2,1)S(1)} %copy.735, s32[]{:T(128)} %constant.235.clone.1, s32[]{:T(128)} %constant.235.clone.1, s32[]{:T(128)} %constant.235.clone.1, s32[]{:T(128)} %constant.249.clone.1) | dynamic-update-slice | bytes 13828 | tf_op jit(solution)/shard_map/scatter | solution.py:97
  864.1 1.4 reshape.433
  865.5 162.9 %all-gather.5.cloned.1.call-done = bf16[128,12,18,34]{3,0,2,1:T(8,128)(2,1)} async-done(((bf16[16,12,18,34]{3,0,2,1:T(8,128)(2,1)}), bf16[128,12,18,34]{3,0,2,1:T(8,128)(2,1)}) %all-gather.5.cloned.1.call-update) | async-done | bytes 1880080 | tf_op jit(solution)/shard_map/all_gather | solution.py:158
  1028.4 4.8 fusion.2
  1034.3 1.9 fusion.10
  1037.2 1.9 fusion.14
  1039.1 1.9 fusion.4
  1040.9 1.9 fusion.8
  1044.1 2.3 add_convert_fusion
  1046.6 1.4 reshape.440
  (185 shorter events, 54.1 us)
Async XLA Ops:
  7.2 503.6 %copy-start = (bf16[3,3,128,128]{3,2,1,0:T(8,128)(2,1)S(1)}, bf16[3,3,128,128]{3,2,1,0:T(8,128)(2,1)}, u32[]{:S(2)}) copy-start(bf16[3,3,128,128]{3,2,1,0:T(8,128)(2,1)} %param.27) | copy-start | bytes 884740
  7.2 300.8 %all-reduce.3.cloned.1.call-start = ((), (), s32[]{:S(2)}) async-start(), calls=%async_computation | async-start | bytes 4194304 | tf_op jit(solution)/shard_map/psum | solution.py:75
  25.7 10.9 %copy-start.17 = (s32[12,4,3]{0,1,2:T(4,128)S(1)}, s32[12,4,3]{0,1,2:T(4,128)}, u32[]{:S(2)}) copy-start(s32[12,4,3]{0,1,2:T(4,128)} %param.28) | copy-start | bytes 1732
  25.7 12.0 %copy-start.26 = (s32[12,4,2]{0,2,1:T(2,128)S(1)}, s32[12,4,2]{0,2,1:T(2,128)}, u32[]{:S(2)}) copy-start(s32[12,4,2]{0,2,1:T(2,128)} %param.29) | copy-start | bytes 1156
  25.7 485.0 %all-gather.3.cloned.1.call-start = ((), (), s32[]{:S(2)}) async-start(), calls=%async_computation.1 | async-start | bytes 7962624 | tf_op jit(solution)/shard_map/all_gather | solution.py:151
  27.0 12.3 %collective-permute-start = (bf16[16,12,16,1]{2,0,3,1:T(8,128)(2,1)S(1)}, bf16[16,12,16,1]{2,0,3,1:T(8,128)(2,1)S(1)}, u32[]{:S(2)}, u32[]{:S(2)}) collective-permute-start(bf16[16,12,16,1]{2,0,3,1:T(8,128)(2,1)S(1)} %copy.684), channel_id=1, source_target_pairs={{0,64},{64,128},{128,192},{1,65},{65,129},{129,193},{2,66},{66,130... | collective-permute-start | bytes 18440 | tf_op jit(solution)/shard_map/ppermute | solution.py:16
  35.3 6.0 collective-permute-start.1
  43.6 5.9 collective-permute-start.2
  45.5 5.4 collective-permute-start.3
  49.5 1.4 copy-start.10
  50.9 0.6 copy-start.12
  53.1 258.7 %copy-start.15 = (pred[12]{0:T(512)(128)(4,1)S(1)}, pred[12]{0:T(512)(128)(4,1)}, u32[]{:S(2)}) copy-start(pred[12]{0:T(512)(128)(4,1)} %get-tuple-element.166) | copy-start | bytes 40
  53.1 259.6 %copy-start.13 = (pred[12]{0:T(512)(128)(4,1)S(1)}, pred[12]{0:T(512)(128)(4,1)}, u32[]{:S(2)}) copy-start(pred[12]{0:T(512)(128)(4,1)} %get-tuple-element.164) | copy-start | bytes 40
  311.0 4.6 copy-start.20
  311.0 4.7 copy-start.11
  311.0 4.9 copy-start.22
  313.8 3.6 copy-start.24
  322.7 2.5 copy-start.18
  345.1 1.0 copy-start.4
  346.1 479.3 %all-reduce.5.cloned.1.call-start = ((), (), s32[]{:S(2)}) async-start(), calls=%async_computation.2 | async-start | bytes 4194304 | tf_op jit(solution)/shard_map/psum | solution.py:75
  510.7 4.8 copy-start.2
  535.1 9.9 copy-start.7
  535.1 10.2 copy-start.6
  536.3 12.1 %collective-permute-start.4 = (bf16[16,12,16,1]{2,0,3,1:T(8,128)(2,1)S(1)}, bf16[16,12,16,1]{2,0,3,1:T(8,128)(2,1)S(1)}, u32[]{:S(2)}, u32[]{:S(2)}) collective-permute-start(bf16[16,12,16,1]{2,0,3,1:T(8,128)(2,1)S(1)} %copy.720), channel_id=1, source_target_pairs={{0,64},{64,128},{128,192},{1,65},{65,129},{129,193},{2,66},{66,130... | collective-permute-start | bytes 18440 | tf_op jit(solution)/shard_map/ppermute | solution.py:16
  539.8 9.9 collective-permute-start.5
  548.4 480.1 %all-gather.5.cloned.1.call-start = ((), (), s32[]{:S(2)}) async-start(), calls=%async_computation.3 | async-start | bytes 7962624 | tf_op jit(solution)/shard_map/all_gather | solution.py:158
  551.1 5.8 collective-permute-start.6
  553.0 5.4 collective-permute-start.7
  556.9 1.5 copy-start.8
  559.1 272.2 %copy-start.16 = (pred[12]{0:T(512)(128)(4,1)S(1)}, pred[12]{0:T(512)(128)(4,1)}, u32[]{:S(2)}) copy-start(pred[12]{0:T(512)(128)(4,1)} %get-tuple-element.166) | copy-start | bytes 40
  559.2 272.4 %copy-start.25 = (pred[12]{0:T(512)(128)(4,1)S(1)}, pred[12]{0:T(512)(128)(4,1)}, u32[]{:S(2)}) copy-start(pred[12]{0:T(512)(128)(4,1)} %get-tuple-element.162) | copy-start | bytes 40
  559.2 272.5 %copy-start.14 = (pred[12]{0:T(512)(128)(4,1)S(1)}, pred[12]{0:T(512)(128)(4,1)}, u32[]{:S(2)}) copy-start(pred[12]{0:T(512)(128)(4,1)} %get-tuple-element.164) | copy-start | bytes 40
  559.2 272.7 %copy-start.23 = (pred[12]{0:T(512)(128)(4,1)S(1)}, pred[12]{0:T(512)(128)(4,1)}, u32[]{:S(2)}) copy-start(pred[12]{0:T(512)(128)(4,1)} %get-tuple-element.161) | copy-start | bytes 40
  828.4 5.5 copy-start.21
  828.5 5.6 copy-start.9
  840.9 1.8 copy-start.19
  842.9 20.9 %copy-start.5 = (bf16[16,12,16,32]{3,0,2,1:T(8,128)(2,1)S(1)}, bf16[16,12,16,32]{3,0,2,1:T(8,128)(2,1)}, u32[]{:S(2)}) copy-start(bf16[16,12,16,32]{3,0,2,1:T(8,128)(2,1)} %get-tuple-element.139) | copy-start | bytes 589828
  862.8 1.0 copy-start.3
  1028.4 4.8 copy-start.1
Sparse Core Ops, SparseCore 0:
  25.8 282.0 all-reduce.2
  346.2 164.4 all-gather.2
  548.5 276.8 all-reduce.4
  863.9 164.4 all-gather.4
where the time goes:
time: 1060 us
  waiting for transfers between devices  850 us (80%)
  local copies, waits for them, and re-layouts  117 us (11%)
  matrix products  36.3 us (3%)
  starting transfers between devices  24 us (2%)
  between operations  15.2 us (1%)
  other arithmetic  12.9 us (1%)
    psum x2, waiting for transfers between devices, face_lines_of(): return lax.psum(contrib.astype(jnp.bfloat16), ('px', 'py'))  521 us
    all_gather x1, waiting for transfers between devices, local(): lax.all_gather(grad_pad, 'ch', axis=0, tiled=True)  163 us
    all_gather x1, waiting for transfers between devices, local(): lax.all_gather(feat_pad, 'ch', axis=0, tiled=True)  163 us
    scatter x2, local copies, waits for them, and re-layouts, pad_field(): padded.at[:, :, :, -1]  36.9 us
  transfers between devices with their start and end apart: 12, of which 7 were waited for; matrix products, arithmetic and copies ran while one was open for 2% of the time, Pallas kernels for 0%

commit v1 on v0

--- a/solution.py
+++ b/solution.py
@@ -72,7 +72,7 @@
         ],
         axis=2,
     )
-    return lax.psum(contrib.astype(jnp.bfloat16), ("px", "py"))
+    return lax.psum(lax.psum(contrib.astype(jnp.bfloat16), "py"), "px")
 
 
 def pad_field(field, edge_table, corner_table):

time: 1060 us -> 838 us (0.79)
  waiting for transfers between devices: 850 us -> 619 us
    psum x2 -> x4, waiting for transfers between devices: 521 us -> 297 us  [face_lines_of(): return lax.psum(lax.psum(contrib.astype(jnp.bfloat16), 'py'), 'px')]
  transfers between devices with their start and end apart: 12 -> 14, of which waited for: 7 -> 9; matrix products, arithmetic and copies ran while one was open for 2% -> 2% of each run, Pallas kernels for 0% -> 0%
where the time goes in v1:
time: 838 us; the launch traced here: 829 us
  waiting for transfers between devices  619 us (74%)
  local copies, waits for them, and re-layouts  118 us (14%)
  matrix products  36.3 us (4%)
  starting transfers between devices  27.3 us (3%)
  between operations  15.6 us (2%)
  other arithmetic  12.9 us (2%)
    psum x4, waiting for transfers between devices, face_lines_of(): return lax.psum(lax.psum(contrib.astype(jnp.bfloat16), 'py'), 'px')  297 us
    all_gather x1, waiting for transfers between devices, local(): lax.all_gather(feat_pad, 'ch', axis=0, tiled=True)  159 us
    all_gather x1, waiting for transfers between devices, local(): lax.all_gather(grad_pad, 'ch', axis=0, tiled=True)  157 us
    scatter x2, local copies, waits for them, and re-layouts, pad_field(): padded.at[:, :, :, -1]  36.9 us
    select_n x12, local copies, waits for them, and re-layouts, placed(): jnp.where(active, lax.dynamic_update_slice_in_dim(blank, values.astype(jn...  20.3 us
    dot_general x9, matrix products, forward_taps(): jnp.einsum('oc,cfab->ofab', taps[tap_row, tap_col], window, preferred_ele...  18.4 us
    dot_general x9, matrix products, backward_taps(): jnp.einsum('oc,ofab->cfab', taps[tap_row, tap_col], window, preferred_ele...  17.9 us
  transfers between devices with their start and end apart: 14, of which 9 were waited for; matrix products, arithmetic and copies ran while one was open for 2% of the time, Pallas kernels for 0%

profile of v1, /device:TPU:8, one launch (start us, length us, event | category | flops | bytes accessed | tf_op | source)
XLA Modules:
  0.0 829.4 jit_solution(11760332068274076259)
XLA Ops:
  11.2 3.0 copy.696
  14.2 1.8 copy.697
  16.0 2.7 select_n.196
  18.7 2.7 select_n.200
  23.0 2.6 copy.698
  27.0 7.1 collective-permute-start
  39.4 1.6 copy.687
  41.2 1.6 copy.689
  43.6 1.9 collective-permute-start.2
  45.5 3.6 collective-permute-start.3
  49.1 50.8 %all-reduce.5.cloned.1.call-done = bf16[16,12,4,128]{1,0,3,2:T(8,128)(2,1)} async-done(((bf16[16,12,4,128]{1,0,3,2:T(8,128)(2,1)}), bf16[16,12,4,128]{1,0,3,2:T(8,128)(2,1)}) %all-reduce.5.cloned.1.call-update) | async-done | bytes 196624 | tf_op jit(solution)/shard_map/psum | solution.py:75
  101.0 1.6 pad_maximum_fusion
  102.7 99.9 %all-reduce.7.cloned.1.call-done = bf16[16,12,4,128]{1,0,3,2:T(8,128)(2,1)} async-done(((bf16[16,12,4,128]{1,0,3,2:T(8,128)(2,1)}), bf16[16,12,4,128]{1,0,3,2:T(8,128)(2,1)}) %all-reduce.7.cloned.1.call-update) | async-done | bytes 196624 | tf_op jit(solution)/shard_map/psum | solution.py:75
  202.6 3.0 copy.702
  213.6 3.8 scatter.30
  221.4 18.3 %scatter.31 = bf16[16,12,18,34]{3,0,2,1:T(8,128)(2,1)S(1)} dynamic-update-slice(bf16[16,12,18,34]{3,0,2,1:T(8,128)(2,1)S(1)} %scatter.30, bf16[16,12,18,1]{3,0,2,1:T(8,128)(2,1)S(1)} %copy.707, s32[]{:T(128)} %constant.235.clone.1, s32[]{:T(128)} %constant.235.clone.1, s32[]{:T(128)} %constant.235.clone.1, s32[]{:T(128)} %constant.249.clone.1) | dynamic-update-slice | bytes 13828 | tf_op jit(solution)/shard_map/scatter | solution.py:97
  241.6 159.3 %all-gather.3.cloned.1.call-done = bf16[128,12,18,34]{3,0,2,1:T(8,128)(2,1)} async-done(((bf16[16,12,18,34]{3,0,2,1:T(8,128)(2,1)}), bf16[128,12,18,34]{3,0,2,1:T(8,128)(2,1)}) %all-gather.3.cloned.1.call-update) | async-done | bytes 1880080 | tf_op jit(solution)/shard_map/all_gather | solution.py:151
  400.9 4.7 fusion.20
  405.8 1.8 fusion.24
  408.5 1.8 fusion.26
  411.2 1.8 fusion.30
  413.1 1.8 fusion.32
  414.9 2.0 fusion.18
  416.8 2.6 fusion.37
  419.4 1.7 convert_select_fusion.1
  421.8 2.3 copy.725
  425.3 1.9 select_n.220
  427.3 1.9 select_n.223
  431.4 2.6 copy.727
  435.3 5.4 collective-permute-start.4
  444.6 3.4 collective-permute-done.5
  449.3 52.0 %all-reduce.9.cloned.1.call-done = bf16[16,12,4,128]{1,0,3,2:T(8,128)(2,1)} async-done(((bf16[16,12,4,128]{1,0,3,2:T(8,128)(2,1)}), bf16[16,12,4,128]{1,0,3,2:T(8,128)(2,1)}) %all-reduce.9.cloned.1.call-update) | async-done | bytes 196624 | tf_op jit(solution)/shard_map/psum | solution.py:75
  501.4 1.9 collective-permute-start.6
  503.4 3.9 collective-permute-start.7
  507.2 1.5 collective-permute-done.7
  509.5 94.4 %all-reduce.11.cloned.1.call-done = bf16[16,12,4,128]{1,0,3,2:T(8,128)(2,1)} async-done(((bf16[16,12,4,128]{1,0,3,2:T(8,128)(2,1)}), bf16[16,12,4,128]{1,0,3,2:T(8,128)(2,1)}) %all-reduce.11.cloned.1.call-update) | async-done | bytes 196624 | tf_op jit(solution)/shard_map/psum | solution.py:75
  603.9 3.0 copy.731
  615.6 3.8 scatter.36
  622.7 18.6 %scatter.39 = bf16[16,12,18,34]{3,0,2,1:T(8,128)(2,1)S(1)} dynamic-update-slice(bf16[16,12,18,34]{3,0,2,1:T(8,128)(2,1)S(1)} %scatter.36, bf16[16,12,18,1]{3,0,2,1:T(8,128)(2,1)S(1)} %copy.735, s32[]{:T(128)} %constant.235.clone.1, s32[]{:T(128)} %constant.235.clone.1, s32[]{:T(128)} %constant.235.clone.1, s32[]{:T(128)} %constant.249.clone.1) | dynamic-update-slice | bytes 13828 | tf_op jit(solution)/shard_map/scatter | solution.py:97
  643.6 1.4 reshape.433
  645.1 157.4 %all-gather.5.cloned.1.call-done = bf16[128,12,18,34]{3,0,2,1:T(8,128)(2,1)} async-done(((bf16[16,12,18,34]{3,0,2,1:T(8,128)(2,1)}), bf16[128,12,18,34]{3,0,2,1:T(8,128)(2,1)}) %all-gather.5.cloned.1.call-update) | async-done | bytes 1880080 | tf_op jit(solution)/shard_map/all_gather | solution.py:158
  802.5 4.8 fusion.2
  808.3 1.9 fusion.10
  811.2 1.9 fusion.14
  813.1 1.9 fusion.4
  815.0 1.9 fusion.8
  818.1 2.3 add_convert_fusion
  820.6 1.4 reshape.440
  (187 shorter events, 58.8 us)
Async XLA Ops:
  7.2 393.8 %copy-start = (bf16[3,3,128,128]{3,2,1,0:T(8,128)(2,1)S(1)}, bf16[3,3,128,128]{3,2,1,0:T(8,128)(2,1)}, u32[]{:S(2)}) copy-start(bf16[3,3,128,128]{3,2,1,0:T(8,128)(2,1)} %param.27) | copy-start | bytes 884740
  7.2 92.8 %all-reduce.5.cloned.1.call-start = ((), (), s32[]{:S(2)}) async-start(), calls=%async_computation | async-start | bytes 4194304 | tf_op jit(solution)/shard_map/psum | solution.py:75
  25.7 10.9 %copy-start.15 = (s32[12,4,3]{0,1,2:T(4,128)S(1)}, s32[12,4,3]{0,1,2:T(4,128)}, u32[]{:S(2)}) copy-start(s32[12,4,3]{0,1,2:T(4,128)} %param.28) | copy-start | bytes 1732
  25.7 12.1 %copy-start.24 = (s32[12,4,2]{0,2,1:T(2,128)S(1)}, s32[12,4,2]{0,2,1:T(2,128)}, u32[]{:S(2)}) copy-start(s32[12,4,2]{0,2,1:T(2,128)} %param.29) | copy-start | bytes 1156
  25.7 176.9 %all-reduce.7.cloned.1.call-start = ((), (), s32[]{:S(2)}) async-start(), calls=%async_computation.1 | async-start | bytes 4194304 | tf_op jit(solution)/shard_map/psum | solution.py:75
  27.0 12.4 %collective-permute-start = (bf16[16,12,16,1]{2,0,3,1:T(8,128)(2,1)S(1)}, bf16[16,12,16,1]{2,0,3,1:T(8,128)(2,1)S(1)}, u32[]{:S(2)}, u32[]{:S(2)}) collective-permute-start(bf16[16,12,16,1]{2,0,3,1:T(8,128)(2,1)S(1)} %copy.684), channel_id=1, source_target_pairs={{0,64},{64,128},{128,192},{1,65},{65,129},{129,193},{2,66},{66,130... | collective-permute-start | bytes 18440 | tf_op jit(solution)/shard_map/ppermute | solution.py:16
  35.3 6.0 collective-permute-start.1
  43.6 56.8 %collective-permute-start.2 = (bf16[16,12,1,34]{3,0,1,2:T(8,128)(2,1)S(1)}, bf16[16,12,1,34]{3,0,1,2:T(8,128)(2,1)S(1)}, u32[]{:S(2)}, u32[]{:S(2)}) collective-permute-start(bf16[16,12,1,34]{3,0,1,2:T(8,128)(2,1)S(1)} %get-tuple-element.148), channel_id=1, source_target_pairs={{0,8},{8,16},{16,24},{24,32},{32,40},{40,48},{48,56},{1,9},{9,17},... | collective-permute-start | bytes 39176 | tf_op jit(solution)/shard_map/ppermute | solution.py:16
  45.5 54.9 %collective-permute-start.3 = (bf16[16,12,1,34]{3,0,1,2:T(8,128)(2,1)S(1)}, bf16[16,12,1,34]{3,0,1,2:T(8,128)(2,1)S(1)}, u32[]{:S(2)}, u32[]{:S(2)}) collective-permute-start(bf16[16,12,1,34]{3,0,1,2:T(8,128)(2,1)S(1)} %get-tuple-element.149), channel_id=1, source_target_pairs={{8,0},{16,8},{24,16},{32,24},{40,32},{48,40},{56,48},{9,1},{17,9},... | collective-permute-start | bytes 39176 | tf_op jit(solution)/shard_map/ppermute | solution.py:17
  100.0 300.9 %all-gather.3.cloned.1.call-start = ((), (), s32[]{:S(2)}) async-start(), calls=%async_computation.2 | async-start | bytes 7962624 | tf_op jit(solution)/shard_map/all_gather | solution.py:151
  100.4 0.6 copy-start.6
  100.4 0.6 copy-start.10
  102.6 103.9 %copy-start.13 = (pred[12]{0:T(512)(128)(4,1)S(1)}, pred[12]{0:T(512)(128)(4,1)}, u32[]{:S(2)}) copy-start(pred[12]{0:T(512)(128)(4,1)} %get-tuple-element.166) | copy-start | bytes 40
  102.6 104.7 %copy-start.11 = (pred[12]{0:T(512)(128)(4,1)S(1)}, pred[12]{0:T(512)(128)(4,1)}, u32[]{:S(2)}) copy-start(pred[12]{0:T(512)(128)(4,1)} %get-tuple-element.164) | copy-start | bytes 40
  102.6 107.6 %copy-start.18 = (pred[12]{0:T(512)(128)(4,1)S(1)}, pred[12]{0:T(512)(128)(4,1)}, u32[]{:S(2)}) copy-start(pred[12]{0:T(512)(128)(4,1)} %get-tuple-element.163) | copy-start | bytes 40
  205.6 4.7 copy-start.7
  205.7 4.8 copy-start.20
  207.5 4.5 copy-start.22
  217.4 2.5 copy-start.16
  220.1 21.1 %copy-start.5 = (bf16[16,12,1,1,512]{4,0,3,2,1:T(8,128)(2,1)S(1)}, bf16[16,12,1,1,512]{4,0,3,2,1:T(8,128)(2,1)}, u32[]{:S(2)}) copy-start(bf16[16,12,1,1,512]{4,0,3,2,1:T(8,128)(2,1)} %param.26) | copy-start | bytes 589828
  239.7 1.0 copy-start.4
  240.8 260.4 %all-reduce.9.cloned.1.call-start = ((), (), s32[]{:S(2)}) async-start(), calls=%async_computation.3 | async-start | bytes 4194304 | tf_op jit(solution)/shard_map/psum | solution.py:75
  400.9 4.8 copy-start.2
  434.1 169.8 %all-reduce.11.cloned.1.call-start = ((), (), s32[]{:S(2)}) async-start(), calls=%async_computation.4 | async-start | bytes 4194304 | tf_op jit(solution)/shard_map/psum | solution.py:75
  435.3 8.0 collective-permute-start.4
  442.0 6.0 collective-permute-start.5
  501.2 301.2 %all-gather.5.cloned.1.call-start = ((), (), s32[]{:S(2)}) async-start(), calls=%async_computation.5 | async-start | bytes 7962624 | tf_op jit(solution)/shard_map/all_gather | solution.py:158
  501.4 5.8 collective-permute-start.6
  503.4 5.4 collective-permute-start.7
  507.2 1.5 copy-start.8
  509.5 100.4 %copy-start.14 = (pred[12]{0:T(512)(128)(4,1)S(1)}, pred[12]{0:T(512)(128)(4,1)}, u32[]{:S(2)}) copy-start(pred[12]{0:T(512)(128)(4,1)} %get-tuple-element.166) | copy-start | bytes 40
  509.5 100.6 %copy-start.23 = (pred[12]{0:T(512)(128)(4,1)S(1)}, pred[12]{0:T(512)(128)(4,1)}, u32[]{:S(2)}) copy-start(pred[12]{0:T(512)(128)(4,1)} %get-tuple-element.162) | copy-start | bytes 40
  509.5 100.7 %copy-start.12 = (pred[12]{0:T(512)(128)(4,1)S(1)}, pred[12]{0:T(512)(128)(4,1)}, u32[]{:S(2)}) copy-start(pred[12]{0:T(512)(128)(4,1)} %get-tuple-element.164) | copy-start | bytes 40
  509.5 100.9 %copy-start.21 = (pred[12]{0:T(512)(128)(4,1)S(1)}, pred[12]{0:T(512)(128)(4,1)}, u32[]{:S(2)}) copy-start(pred[12]{0:T(512)(128)(4,1)} %get-tuple-element.161) | copy-start | bytes 40
  606.9 5.5 copy-start.19
  606.9 5.6 copy-start.9
  619.4 1.8 copy-start.17
  641.3 1.0 copy-start.3
  802.5 4.8 copy-start.1
Sparse Core Ops, SparseCore 0:
  25.8 74.1 all-reduce.4
  102.6 99.9 all-reduce.6
  240.9 159.9 all-gather.2
  434.2 66.9 all-reduce.8
  503.9 99.9 all-reduce.10
  642.4 159.9 all-gather.4
